TPU v7x, 32 devices: a whole 2x2x4 slice. The times are simulated.
32 devices in a mesh: seq: 8 (over y, x, core), tp: 4 (over z).
Axes of the slice: x: 2, y: 2, z: 4, core: 2. Of those that a mesh axis runs over, the one named last changes fastest.
Arguments:
- grad_out: bfloat16 [1024, 8192], P('seq', 'tp'), may hold values from -6 to 6
- resid_in: bfloat16 [1024, 8192], P('seq', 'tp'), may hold values from -6 to 6
- down_weight: bfloat16 [28672, 8192], P('seq', 'tp'), may hold values from -0.03125 to 0.03125
- hidden_clean: bfloat16 [28672, 512], P('seq', 'tp'), may hold values from -6 to 6
- hidden_corrupt: bfloat16 [28672, 512], P('seq', 'tp'), may hold values from -6 to 6
- patched: int32 [14336], replicated, may hold values from 0 to 28671, as said below
Outputs:
- resid_scores: float32 [1024], P('seq')
- token_scores: float32 [512], P('tp')
- neuron_scores: float32 [28672], P('seq')
Inputs may be any that keep to these rules, and one draw needn't show every extreme that they name: `patched`: 14336 distinct hidden-unit indices.
All inputs are finite; a program needn't handle non-finite values.
Results may differ from a plain program's by a relative error of at most 0.0046.
Values may be sent and summed in bfloat16 or wider, within the bound.
A program may use at most 128 MiB of HBM per device.

v0:
```python
import math
import jax
import jax.numpy as jnp
from jax import lax
from jax.sharding import PartitionSpec as P


def from_behind(value, axis, steps):
    count = lax.axis_size(axis)
    pairs = [(source, (source + steps) % count) for source in range(count)]
    return lax.ppermute(value, axis, pairs)


def patch_mask(patched, unit_rows):
    lanes = math.gcd(unit_rows, 128)
    groups = unit_rows // lanes
    local = patched - lax.axis_index("seq") * unit_rows
    high = local[None, :] // lanes == jnp.arange(groups, dtype=jnp.int32)[:, None]
    high = high & (local >= 0)[None, :]
    low = (local % lanes)[:, None] == jnp.arange(lanes, dtype=jnp.int32)[None, :]
    counts = lax.dot_general(
        high.astype(jnp.bfloat16),
        low.astype(jnp.bfloat16),
        (((1,), (0,)), ((), ())),
        preferred_element_type=jnp.float32,
    )
    return counts.reshape(unit_rows)


def shards(grad_out, resid_in, down_weight, hidden_clean, hidden_corrupt, patched):
    seq_count = lax.axis_size("seq")
    tp_count = lax.axis_size("tp")
    pair_count = seq_count // 2
    half_rows = grad_out.shape[0] // 2
    unit_rows = down_weight.shape[0]
    model_width = resid_in.shape[1] * tp_count
    hidden_diff = (hidden_clean.astype(jnp.float32) - hidden_corrupt.astype(jnp.float32)).astype(
        jnp.bfloat16
    )
    diff_all = lax.all_gather(hidden_diff, "tp", axis=0)
    in_upper = lax.axis_index("seq") // pair_count
    send_start = (1 - in_upper) * half_rows
    keep_start = in_upper * half_rows
    sent_grad = lax.dynamic_slice_in_dim(grad_out, send_start, half_rows, 0)
    partner_grad = from_behind(sent_grad, "seq", pair_count)
    partner_resid = from_behind(resid_in, "seq", pair_count)
    sign_factor = (1 - 2 * in_upper).astype(jnp.float32)
    resid_diff = sign_factor * (resid_in.astype(jnp.float32) - partner_resid.astype(jnp.float32))
    resid_part = jnp.sum(resid_diff * grad_out.astype(jnp.float32), axis=1)
    kept_grad = lax.dynamic_slice_in_dim(grad_out, keep_start, half_rows, 0)
    grad_mean = ((kept_grad.astype(jnp.float32) + partner_grad.astype(jnp.float32)) * 0.5).astype(
        jnp.bfloat16
    )
    grads = lax.all_gather(grad_mean, "seq", axis=0)
    width = grads.shape[-1]
    grads = grads.reshape(2, pair_count, half_rows, width).transpose(1, 0, 2, 3)
    grads = grads.reshape(-1, width)
    total_len = grads.shape[0]
    in_patch = patch_mask(patched, unit_rows)
    unit_grad = lax.dot_general(
        down_weight, grads, (((1,), (1,)), ((), ())), preferred_element_type=jnp.float32
    )
    local_len = total_len // tp_count
    token_parts = []
    unit_part = 0.0
    for block in range(tp_count):
        part = unit_grad[:, block * local_len : (block + 1) * local_len]
        product = diff_all[block].astype(jnp.float32) * part
        token_parts.append(jnp.sum(product * in_patch[:, None], axis=0))
        unit_part = unit_part + jnp.sum(product, axis=1)
    token_part = jnp.stack(token_parts)
    token_total = lax.psum(token_part, ("seq", "tp"))
    token_mine = lax.dynamic_index_in_dim(token_total, lax.axis_index("tp"), 0, keepdims=False)
    token_scores = token_mine / math.sqrt(patched.shape[0])
    unit_total, resid_total = lax.psum((unit_part, resid_part), "tp")
    neuron_scores = unit_total / math.sqrt(total_len)
    resid_scores = resid_total / math.sqrt(model_width)
    return (resid_scores, token_scores, neuron_scores)


def solution(mesh):
    in_specs = (P("seq", "tp"), P("seq", "tp"), P("seq", "tp"), P("seq", "tp"), P("seq", "tp"), P())
    out_specs = (P("seq"), P("tp"), P("seq"))
    return jax.shard_map(shards, mesh=mesh, in_specs=in_specs, out_specs=out_specs, check_vma=False)
```

profile of v0, /device:TPU:10, one launch (start us, length us, event | category | flops | bytes accessed | tf_op | source)
XLA Modules:
  0.0 192.9 jit_solution(12017848095058334556)
XLA Ops:
  7.3 1.1 constant_dynamic-slice_fusion.1
  8.3 1.6 collective-permute-start.1
  9.9 6.5 %collective-permute-done.1 = bf16[64,2048]{1,0:T(8,128)(2,1)S(1)} collective-permute-done((bf16[64,2048]{1,0:T(8,128)(2,1)S(1)}, bf16[64,2048]{1,0:T(8,128)(2,1)S(1)}, u32[]{:S(2)}, u32[]{:S(2)}) %collective-permute-start.1) | collective-permute-done | bytes 262176 | tf_op jit(solution)/shard_map/ppermute | solution.py:11
  16.5 1.8 multiply_convert_fusion
  18.2 0.0 all-gather.5.cloned.1.call-start
  18.3 1.6 collective-permute-start
  19.9 0.5 copy.14
  20.4 0.5 copy.13
  20.9 1.1 subtract_convert_fusion
  22.1 0.1 add_select_fusion.1
  22.2 0.3 fusion.22
  22.6 2.1 %fusion.8 = f32[3584]{0:T(1024)S(1)} fusion(s32[14336]{0:T(1024)S(1)} %get-tuple-element.18, pred[28,14336]{1,0:T(8,128)(4,1)S(1)} %fusion.22), kind=kOutput, calls=%fused_computation.19 | convolution fusion | flops 104595456 | bytes 473088 | tf_op jit(solution)/shard_map/dot_general | solution.py:21
  24.7 9.5 %collective-permute-done = bf16[128,2048]{1,0:T(8,128)(2,1)S(1)} collective-permute-done((bf16[128,2048]{1,0:T(8,128)(2,1)}, bf16[128,2048]{1,0:T(8,128)(2,1)S(1)}, u32[]{:S(2)}, u32[]{:S(2)}) %collective-permute-start) | collective-permute-done | bytes 524320 | tf_op jit(solution)/shard_map/ppermute | solution.py:11
  34.2 0.3 multiply_reduce_fusion.4
  34.5 14.7 %all-gather.7.cloned.1.call-done = bf16[512,2048]{1,0:T(8,128)(2,1)} async-done(((bf16[64,2048]{1,0:T(8,128)(2,1)}), bf16[512,2048]{1,0:T(8,128)(2,1)}) %all-gather.7.cloned.1.call-update) | async-done | bytes 2097168 | tf_op jit(solution)/shard_map/all_gather | solution.py:54
  49.2 1.7 copy.15
  51.0 13.1 %convolution_bitcast_fusion = f32[3584,512]{0,1:T(8,128)} fusion(bf16[512,2048]{1,0:T(8,128)(2,1)S(1)} %bitcast.20, bf16[3584,2048]{1,0:T(8,128)(2,1)} %param.8), kind=kOutput, calls=%fused_computation.2 | convolution fusion | flops 7516192768 | bytes 24117248 | tf_op jit(solution)/shard_map/dot_general | solution.py:60
  64.1 56.5 %all-gather.5.cloned.1.call-done = bf16[14336,128]{0,1:T(8,128)(2,1)} async-done(((bf16[3584,128]{0,1:T(8,128)(2,1)}), bf16[14336,128]{0,1:T(8,128)(2,1)}) %all-gather.5.cloned.1.call-update) | async-done | bytes 3670032 | tf_op jit(solution)/shard_map/all_gather | solution.py:40
  120.5 4.9 %fusion.5 = (f32[3584]{0:T(1024)S(1)}, f32[3584]{0:T(1024)S(1)}, f32[3584]{0:T(1024)S(1)}, f32[3584]{0:T(1024)S(1)}, f32[128]{0:T(128)S(1)}, /*index=5*/f32[128]{0:T(128)S(1)}, f32[128]{0:T(128)S(1)}, f32[128]{0:T(128)S(1)}) fusion(f32[3584,512]{0,1:T(8,128)} %convolution_bitcast_fusion, bf16[14336,128]{0,1:T(8,128)(2,1)} %all-gather.5.cloned.1.call-done, ...), kind=kLoop, calls=%fused_computation.16 | loop fusion | flops 9160192 | bytes 11083776 | tf_op jit(solution)/shard_map/reduce_sum | solution.py:70
  125.4 16.7 %all-reduce = (f32[128]{0:T(128)S(1)}, f32[3584]{0:T(1024)S(1)}) all-reduce(f32[128]{0:T(128)S(1)} %multiply_reduce_fusion.4, f32[3584]{0:T(1024)S(1)} %add_add_fusion), channel_id=1, replica_groups=mesh['seq'=8,'tp'=4] {'tp'}, use_global_device_ids=true, to_apply=%region_1.2 | all-reduce | flops 3712 | bytes 29696 | tf_op jit(solution)/shard_map/psum | solution.py:75
  142.1 0.5 broadcast_multiply_fusion.1
  142.7 42.3 %psum.22 = f32[4,128]{1,0:T(4,128)S(1)} all-reduce(f32[4,128]{1,0:T(4,128)S(1)} %pad_maximum_fusion), channel_id=1, replica_groups=mesh['seq'=8,'tp'=4] {'seq','tp'}, use_global_device_ids=true, to_apply=%region_6.7 | all-reduce | flops 512 | bytes 4096 | tf_op jit(solution)/shard_map/psum | solution.py:72
  185.0 0.6 broadcast_multiply_fusion
  185.6 0.5 fusion.16
  (16 shorter events, 0.1 us)
Async XLA Ops:
  7.2 12.7 %copy-start.1 = (bf16[3584,128]{1,0:T(8,128)(2,1)S(1)}, bf16[3584,128]{1,0:T(8,128)(2,1)}, u32[]{:S(2)}) copy-start(bf16[3584,128]{1,0:T(8,128)(2,1)} %param.10) | copy-start | bytes 2752516
  7.2 13.2 %copy-start.2 = (bf16[3584,128]{1,0:T(8,128)(2,1)S(1)}, bf16[3584,128]{1,0:T(8,128)(2,1)}, u32[]{:S(2)}) copy-start(bf16[3584,128]{1,0:T(8,128)(2,1)} %param.9) | copy-start | bytes 2752516
  7.2 42.0 %all-gather.7.cloned.1.call-start = ((), (), s32[]{:S(2)}) async-start(), calls=%async_computation.1 | async-start | bytes 2359296 | tf_op jit(solution)/shard_map/all_gather | solution.py:54
  8.3 8.1 %collective-permute-start.1 = (bf16[64,2048]{1,0:T(8,128)(2,1)S(1)}, bf16[64,2048]{1,0:T(8,128)(2,1)S(1)}, u32[]{:S(2)}, u32[]{:S(2)}) collective-permute-start(bf16[64,2048]{1,0:T(8,128)(2,1)S(1)} %constant_dynamic-slice_fusion.1), channel_id=1, source_target_pairs={{0,16},{4,20},{8,24},{12,28},{16,0},{20,4},{24,8},{28,12},{1,17},{... | collective-permute-start | bytes 786440 | tf_op jit(solution)/shard_map/ppermute | solution.py:11
  18.2 102.3 %all-gather.5.cloned.1.call-start = ((), (), s32[]{:S(2)}) async-start(), calls=%async_computation | async-start | bytes 4587520 | tf_op jit(solution)/shard_map/all_gather | solution.py:40
  18.3 15.9 %collective-permute-start = (bf16[128,2048]{1,0:T(8,128)(2,1)}, bf16[128,2048]{1,0:T(8,128)(2,1)S(1)}, u32[]{:S(2)}, u32[]{:S(2)}) collective-permute-start(bf16[128,2048]{1,0:T(8,128)(2,1)} %param.7), channel_id=1, source_target_pairs={{0,16},{4,20},{8,24},{12,28},{16,0},{20,4},{24,8},{28,12},{1,17},{... | collective-permute-start | bytes 1572872 | tf_op jit(solution)/shard_map/ppermute | solution.py:11
  20.9 1.2 copy-start.4
  22.2 12.0 %copy-start = (bf16[128,2048]{1,0:T(8,128)(2,1)S(1)}, bf16[128,2048]{1,0:T(8,128)(2,1)}, u32[]{:S(2)}) copy-start(bf16[128,2048]{1,0:T(8,128)(2,1)} %param.6) | copy-start | bytes 1572868
  22.2 11.9 %copy-start.3 = (bf16[128,2048]{1,0:T(8,128)(2,1)S(1)}, bf16[128,2048]{1,0:T(8,128)(2,1)}, u32[]{:S(2)}) copy-start(bf16[128,2048]{1,0:T(8,128)(2,1)} %param.7) | copy-start | bytes 1572868
Sparse Core Ops, SparseCore 0:
  18.4 30.8 all-gather.6
  50.8 69.7 all-gather.4
where the time goes:
time: 193 us
  waiting for transfers between devices  87.2 us (45%)
  blocking collectives  59 us (31%)
  matrix products  15.2 us (8%)
  between operations  14.2 us (7%)
  other arithmetic  10.2 us (5%)
  local copies, waits for them, and re-layouts  3.87 us (2%)
  starting transfers between devices  3.25 us (2%)
    all_gather x1, waiting for transfers between devices, shards(): diff_all = lax.all_gather(hidden_diff, 'tp', axis=0)  56.5 us
    psum x1, blocking collectives, shards(): token_total = lax.psum(token_part, ('seq', 'tp'))  42.3 us
    psum x1, blocking collectives, shards(): unit_total, resid_total = lax.psum((unit_part, resid_part), 'tp')  16.7 us
    ppermute x2, waiting for transfers between devices, from_behind(): return lax.ppermute(value, axis, pairs)  16 us
    all_gather x1, waiting for transfers between devices, shards(): grads = lax.all_gather(grad_mean, 'seq', axis=0)  14.7 us
    dot_general x1, matrix products, shards(): lax.dot_general(down_weight, grads, (((1,), (1,)), ((), ())), preferred_e...  13.1 us
    reduce_sum x1, other arithmetic, shards(): unit_part = unit_part + jnp.sum(product, axis=1)  4.87 us
  transfers between devices with their start and end apart: 4, of which 4 were waited for; matrix products, arithmetic and copies ran while one was open for 10% of the time, Pallas kernels for 0%

commit v1 on v0

--- a/solution.py
+++ b/solution.py
@@ -69,7 +69,7 @@
         token_parts.append(jnp.sum(product * in_patch[:, None], axis=0))
         unit_part = unit_part + jnp.sum(product, axis=1)
     token_part = jnp.stack(token_parts)
-    token_total = lax.psum(token_part, ("seq", "tp"))
+    token_total = lax.psum(lax.psum(token_part, "tp"), "seq")
     token_mine = lax.dynamic_index_in_dim(token_total, lax.axis_index("tp"), 0, keepdims=False)
     token_scores = token_mine / math.sqrt(patched.shape[0])
     unit_total, resid_total = lax.psum((unit_part, resid_part), "tp")

time: 193 us -> 166 us (0.86)
  the two profiles are of different devices: /device:TPU:10 before, /device:TPU:0 now
where the time goes in v1:
time: 166 us
  waiting for transfers between devices  89.5 us (54%)
  blocking collectives  28.1 us (17%)
  matrix products  15.2 us (9%)
  between operations  14.2 us (9%)
  other arithmetic  10.2 us (6%)
  starting transfers between devices  4.92 us (3%)
  local copies, waits for them, and re-layouts  3.87 us (2%)
    all_gather x1, waiting for transfers between devices, shards(): diff_all = lax.all_gather(hidden_diff, 'tp', axis=0)  58.9 us
    psum x1, blocking collectives, shards(): unit_total, resid_total = lax.psum((unit_part, resid_part), 'tp')  16.3 us
    ppermute x2, waiting for transfers between devices, from_behind(): return lax.ppermute(value, axis, pairs)  15.9 us
    all_gather x1, waiting for transfers between devices, shards(): grads = lax.all_gather(grad_mean, 'seq', axis=0)  14.7 us
    dot_general x1, matrix products, shards(): lax.dot_general(down_weight, grads, (((1,), (1,)), ((), ())), preferred_e...  13.1 us
    psum x1, blocking collectives, shards(): token_total = lax.psum(lax.psum(token_part, 'tp'), 'seq')  11.8 us
    reduce_sum x1, other arithmetic, shards(): unit_part = unit_part + jnp.sum(product, axis=1)  4.87 us
    ppermute x2, starting transfers between devices, from_behind(): return lax.ppermute(value, axis, pairs)  4.84 us
  transfers between devices with their start and end apart: 4, of which 4 were waited for; matrix products, arithmetic and copies ran while one was open for 12% of the time, Pallas kernels for 0%

profile of v1, /device:TPU:0, one launch (start us, length us, event | category | flops | bytes accessed | tf_op | source)
XLA Modules:
  0.0 166.0 jit_solution(5245824860959487487)
XLA Ops:
  7.3 1.1 constant_dynamic-slice_fusion.1
  8.3 3.0 %collective-permute-start.1 = (bf16[64,2048]{1,0:T(8,128)(2,1)S(1)}, bf16[64,2048]{1,0:T(8,128)(2,1)S(1)}, u32[]{:S(2)}, u32[]{:S(2)}) collective-permute-start(bf16[64,2048]{1,0:T(8,128)(2,1)S(1)} %constant_dynamic-slice_fusion.1), channel_id=1, source_target_pairs={{0,16},{4,20},{8,24},{12,28},{16,0},{20,4},{24,8},{28,12},{1,17},{... | collective-permute-start | bytes 786440 | tf_op jit(solution)/shard_map/ppermute | solution.py:11
  11.4 6.3 %collective-permute-done.1 = bf16[64,2048]{1,0:T(8,128)(2,1)S(1)} collective-permute-done((bf16[64,2048]{1,0:T(8,128)(2,1)S(1)}, bf16[64,2048]{1,0:T(8,128)(2,1)S(1)}, u32[]{:S(2)}, u32[]{:S(2)}) %collective-permute-start.1) | collective-permute-done | bytes 262176 | tf_op jit(solution)/shard_map/ppermute | solution.py:11
  17.7 1.8 %multiply_convert_fusion = bf16[64,2048]{1,0:T(8,128)(2,1)} fusion(bf16[64,2048]{1,0:T(8,128)(2,1)S(1)} %collective-permute-done.1, bf16[128,2048]{1,0:T(8,128)(2,1)} %param.6, s32[]{:T(128)S(6)} %select_n.28), kind=kLoop, calls=%fused_computation.23 | loop fusion | flops 655360 | bytes 786436 | tf_op jit(solution)/shard_map/convert_element_type | solution.py:51
  19.5 0.0 all-gather.5.cloned.1.call-start
  19.5 1.8 %collective-permute-start = (bf16[128,2048]{1,0:T(8,128)(2,1)}, bf16[128,2048]{1,0:T(8,128)(2,1)S(1)}, u32[]{:S(2)}, u32[]{:S(2)}) collective-permute-start(bf16[128,2048]{1,0:T(8,128)(2,1)} %param.7), channel_id=1, source_target_pairs={{0,16},{4,20},{8,24},{12,28},{16,0},{20,4},{24,8},{28,12},{1,17},{... | collective-permute-start | bytes 1572872 | tf_op jit(solution)/shard_map/ppermute | solution.py:11
  21.3 0.5 copy.14
  21.9 0.5 copy.13
  22.4 1.1 subtract_convert_fusion
  23.6 0.1 add_select_fusion.1
  23.7 0.3 fusion.22
  24.0 2.1 %fusion.8 = f32[3584]{0:T(1024)S(1)} fusion(s32[14336]{0:T(1024)S(1)} %get-tuple-element.19, pred[28,14336]{1,0:T(8,128)(4,1)S(1)} %fusion.22), kind=kOutput, calls=%fused_computation.19 | convolution fusion | flops 104595456 | bytes 473088 | tf_op jit(solution)/shard_map/dot_general | solution.py:21
  26.1 9.6 %collective-permute-done = bf16[128,2048]{1,0:T(8,128)(2,1)S(1)} collective-permute-done((bf16[128,2048]{1,0:T(8,128)(2,1)}, bf16[128,2048]{1,0:T(8,128)(2,1)S(1)}, u32[]{:S(2)}, u32[]{:S(2)}) %collective-permute-start) | collective-permute-done | bytes 524320 | tf_op jit(solution)/shard_map/ppermute | solution.py:11
  35.7 0.4 multiply_reduce_fusion.4
  36.1 14.7 %all-gather.7.cloned.1.call-done = bf16[512,2048]{1,0:T(8,128)(2,1)} async-done(((bf16[64,2048]{1,0:T(8,128)(2,1)}), bf16[512,2048]{1,0:T(8,128)(2,1)}) %all-gather.7.cloned.1.call-update) | async-done | bytes 2097168 | tf_op jit(solution)/shard_map/all_gather | solution.py:54
  50.8 1.7 %copy.15 = bf16[4,2,64,2048]{3,2,1,0:T(8,128)(2,1)S(1)} copy(bf16[4,2,64,2048]{3,2,0,1:T(8,128)(2,1)} %bitcast.19) | data formatting | bytes 4194304 | tf_op jit(solution)/shard_map/transpose | solution.py:56
  52.5 13.1 %convolution_bitcast_fusion = f32[3584,512]{0,1:T(8,128)} fusion(bf16[512,2048]{1,0:T(8,128)(2,1)S(1)} %bitcast.20, bf16[3584,2048]{1,0:T(8,128)(2,1)} %param.8), kind=kOutput, calls=%fused_computation.2 | convolution fusion | flops 7516192768 | bytes 24117248 | tf_op jit(solution)/shard_map/dot_general | solution.py:60
  65.6 58.9 %all-gather.5.cloned.1.call-done = bf16[14336,128]{0,1:T(8,128)(2,1)} async-done(((bf16[3584,128]{0,1:T(8,128)(2,1)}), bf16[14336,128]{0,1:T(8,128)(2,1)}) %all-gather.5.cloned.1.call-update) | async-done | bytes 3670032 | tf_op jit(solution)/shard_map/all_gather | solution.py:40
  124.5 4.9 %fusion.5 = (f32[3584]{0:T(1024)S(1)}, f32[3584]{0:T(1024)S(1)}, f32[3584]{0:T(1024)S(1)}, f32[3584]{0:T(1024)S(1)}, f32[128]{0:T(128)S(1)}, /*index=5*/f32[128]{0:T(128)S(1)}, f32[128]{0:T(128)S(1)}, f32[128]{0:T(128)S(1)}) fusion(f32[3584,512]{0,1:T(8,128)} %convolution_bitcast_fusion, bf16[14336,128]{0,1:T(8,128)(2,1)} %all-gather.5.cloned.1.call-done, ...), kind=kLoop, calls=%fused_computation.16 | loop fusion | flops 9160192 | bytes 11083776 | tf_op jit(solution)/shard_map/reduce_sum | solution.py:70
  129.4 16.3 %all-reduce = (f32[128]{0:T(128)S(1)}, f32[4,128]{1,0:T(4,128)S(1)}, f32[3584]{0:T(1024)S(1)}) all-reduce(f32[128]{0:T(128)S(1)} %multiply_reduce_fusion.4, f32[4,128]{1,0:T(4,128)S(1)} %pad_maximum_fusion, f32[3584]{0:T(1024)S(1)} %add_add_fusion), channel_id=1, replica_groups=mesh['seq'=8,'tp'=4] {'tp'}, use_global_device_ids=true, to_apply=%region_1.2 | all-reduce | flops 4224 | bytes 33792 | tf_op jit(solution)/shard_map/psum | solution.py:75
  145.7 0.5 broadcast_multiply_fusion.1
  146.2 11.8 %psum.30 = f32[4,128]{1,0:T(4,128)S(1)} all-reduce(f32[4,128]{1,0:T(4,128)S(1)} %get-tuple-element.16), channel_id=1, replica_groups=mesh['seq'=8,'tp'=4] {'seq'}, use_global_device_ids=true, to_apply=%region_7.8 | all-reduce | flops 512 | bytes 4096 | tf_op jit(solution)/shard_map/psum | solution.py:72
  158.0 0.6 broadcast_multiply_fusion
  158.6 0.5 fusion.16
  (16 shorter events, 0.1 us)
Async XLA Ops:
  7.2 14.2 %copy-start.1 = (bf16[3584,128]{1,0:T(8,128)(2,1)S(1)}, bf16[3584,128]{1,0:T(8,128)(2,1)}, u32[]{:S(2)}) copy-start(bf16[3584,128]{1,0:T(8,128)(2,1)} %param.10) | copy-start | bytes 2752516
  7.2 14.7 %copy-start.2 = (bf16[3584,128]{1,0:T(8,128)(2,1)S(1)}, bf16[3584,128]{1,0:T(8,128)(2,1)}, u32[]{:S(2)}) copy-start(bf16[3584,128]{1,0:T(8,128)(2,1)} %param.9) | copy-start | bytes 2752516
  7.2 43.6 %all-gather.7.cloned.1.call-start = ((), (), s32[]{:S(2)}) async-start(), calls=%async_computation.1 | async-start | bytes 2359296 | tf_op jit(solution)/shard_map/all_gather | solution.py:54
  8.3 9.3 %collective-permute-start.1 = (bf16[64,2048]{1,0:T(8,128)(2,1)S(1)}, bf16[64,2048]{1,0:T(8,128)(2,1)S(1)}, u32[]{:S(2)}, u32[]{:S(2)}) collective-permute-start(bf16[64,2048]{1,0:T(8,128)(2,1)S(1)} %constant_dynamic-slice_fusion.1), channel_id=1, source_target_pairs={{0,16},{4,20},{8,24},{12,28},{16,0},{20,4},{24,8},{28,12},{1,17},{... | collective-permute-start | bytes 786440 | tf_op jit(solution)/shard_map/ppermute | solution.py:11
  19.5 105.0 %all-gather.5.cloned.1.call-start = ((), (), s32[]{:S(2)}) async-start(), calls=%async_computation | async-start | bytes 4587520 | tf_op jit(solution)/shard_map/all_gather | solution.py:40
  19.5 16.2 %collective-permute-start = (bf16[128,2048]{1,0:T(8,128)(2,1)}, bf16[128,2048]{1,0:T(8,128)(2,1)S(1)}, u32[]{:S(2)}, u32[]{:S(2)}) collective-permute-start(bf16[128,2048]{1,0:T(8,128)(2,1)} %param.7), channel_id=1, source_target_pairs={{0,16},{4,20},{8,24},{12,28},{16,0},{20,4},{24,8},{28,12},{1,17},{... | collective-permute-start | bytes 1572872 | tf_op jit(solution)/shard_map/ppermute | solution.py:11
  22.4 1.2 copy-start.4
  23.7 12.1 %copy-start = (bf16[128,2048]{1,0:T(8,128)(2,1)S(1)}, bf16[128,2048]{1,0:T(8,128)(2,1)}, u32[]{:S(2)}) copy-start(bf16[128,2048]{1,0:T(8,128)(2,1)} %param.6) | copy-start | bytes 1572868
  23.7 12.0 %copy-start.3 = (bf16[128,2048]{1,0:T(8,128)(2,1)S(1)}, bf16[128,2048]{1,0:T(8,128)(2,1)}, u32[]{:S(2)}) copy-start(bf16[128,2048]{1,0:T(8,128)(2,1)} %param.7) | copy-start | bytes 1572868
Sparse Core Ops, SparseCore 0:
  19.6 31.1 all-gather.6
  52.4 72.1 all-gather.4
